TPU v7x, 1024 devices: a whole 8x8x8 slice. The times are simulated.
1024 devices in a mesh: aisle: 32 (over x, z_hi, core), row: 32 (over y, z_lo).
Axes of the slice: x: 8, y: 8, z: 8 (z_hi: 2, z_lo: 4; z = z_hi * 4 + z_lo), core: 2. Of those that a mesh axis runs over, the one named last changes fastest.
Arguments:
- source: float32 [8, 512, 4096], P(None, 'row', 'aisle'), may hold values from -6 to 6
- conduct: float32 [8, 512, 4096], P(None, 'row', 'aisle'), may hold values from 1 to 10
- solid: int32 [8, 512, 4096], P(None, 'row', 'aisle'), may hold values 0 or 1
Outputs:
- correction: float32 [8, 512, 4096], P(None, 'row', 'aisle')
All inputs are finite; a program needn't handle non-finite values. No bound on the sum of `solid` on one device may be relied on, other than what follows from the above.
Results may differ from a plain program's by a relative error of at most 0.0003.
Values sent between devices are 32-bit elements; how exact they have to be, the bound alone decides.
A program may use at most 32 MiB of HBM per device.

v0:
```python
import jax
import jax.numpy as jnp
from jax import lax
from jax.sharding import PartitionSpec as P

OV = 2
SWEEPS = 6


lower_end = 0.2
upper_end = 2.0


def shifted(block, axis, distance):
    devices = range(lax.axis_size(axis))
    route = [((i - distance) % len(devices), i) for i in devices]
    return lax.ppermute(block, axis, route)


def from_behind(shard, axis, by):
    count = lax.axis_size(axis)
    pairs = [(i, i + by) for i in range(count) if 0 <= i + by < count]
    return lax.ppermute(shard, axis, pairs)


def extended_2(block, sides, width):
    for axis, dim in sides:
        count = lax.axis_size(axis)
        forward = [(i, i + 1) for i in range(count - 1)]
        forward.append((count - 1, 0))
        backward = [(target, source) for source, target in forward]
        low = lax.ppermute(
            lax.slice_in_dim(block, block.shape[dim] - width, None, axis=dim), axis, forward
        )
        high = lax.ppermute(lax.slice_in_dim(block, 0, width, axis=dim), axis, backward)
        block = jnp.concatenate([low, block, high], axis=dim)
    return block


def padded(values):
    return jnp.pad(values, [(0, 0)] * (values.ndim - 3) + [(1, 1)] * 3)


def beside(padded_values):
    return [
        padded_values[..., 2:, 1:-1, 1:-1],
        padded_values[..., :-2, 1:-1, 1:-1],
        padded_values[..., 1:-1, 2:, 1:-1],
        padded_values[..., 1:-1, :-2, 1:-1],
        padded_values[..., 1:-1, 1:-1, 2:],
        padded_values[..., 1:-1, 1:-1, :-2],
    ]


def coupling(padded_cond, shift_term):
    centre = padded_cond[..., 1:-1, 1:-1, 1:-1]
    weights = [0.5 * (centre + other) for other in beside(padded_cond)]
    diagonal = shift_term
    for weight in weights:
        diagonal = diagonal + weight
    return (weights, diagonal)


def operate(padded_values, weights, diagonal):
    others = beside(padded_values)
    summed = weights[0] * others[0]
    for number in range(1, 6):
        summed = summed + weights[number] * others[number]
    return diagonal * padded_values[..., 1:-1, 1:-1, 1:-1] - summed


def smooth_local(source_ext, weights, diagonal):
    middle = 0.5 * (upper_end + lower_end)
    spread = 0.5 * (upper_end - lower_end)
    ratio_now = spread / middle
    inverse = 1.0 / diagonal
    update = inverse * source_ext / middle
    estimate = update
    for sweep_no in range(SWEEPS):
        remain = source_ext - operate(padded(estimate), weights, diagonal)
        ratio_next = 1.0 / (2.0 * middle / spread - ratio_now)
        update = ratio_next * ratio_now * update + 2.0 * ratio_next / spread * inverse * remain
        estimate = estimate + update
        ratio_now = ratio_next
    return estimate


def aisle_pass(slab, offset):
    return shifted(slab, "aisle", offset)


def row_pass(slab, offset):
    return from_behind(slab, "row", offset)


def fold_aisle(result):
    inner = result[..., OV:-OV]
    from_lower = aisle_pass(result[..., -OV:], 1)
    from_upper = aisle_pass(result[..., :OV], -1)
    return jnp.concatenate(
        [inner[..., :OV] + from_lower, inner[..., OV:-OV], inner[..., -OV:] + from_upper], axis=2
    )


def fold_row(result):
    inner = result[:, OV:-OV, :]
    from_lower = row_pass(result[:, -OV:, :], 1)
    from_upper = row_pass(result[:, :OV, :], -1)
    return jnp.concatenate(
        [inner[:, :OV, :] + from_lower, inner[:, OV:-OV, :], inner[:, -OV:, :] + from_upper], axis=1
    )


def schwarz_apply(source_core, weights, diagonal):
    source_ext = jnp.pad(source_core, ((0, 0), (OV, OV), (OV, OV)))
    result = smooth_local(source_ext, weights, diagonal)
    return fold_row(fold_aisle(result))


def body(source, conduct, solid):
    rows_here = source.shape[1]
    cols_here = source.shape[2]
    row_count = lax.axis_size("row")
    row_place = lax.axis_index("row")
    shift_term = 0.05 + 20.0 * solid.astype(jnp.float32)
    stacked = jnp.stack([conduct, shift_term])
    extended = extended_2(stacked, (("aisle", 3), ("row", 2)), OV)
    global_row = row_place * rows_here - OV + lax.iota(jnp.int32, rows_here + 2 * OV)
    outside = ((global_row < 0) | (global_row >= rows_here * row_count))[None, :, None]
    cond_ext = jnp.where(outside, 0.0, extended[0])
    shift_ext = jnp.where(outside, 1.0, extended[1])
    weights, diagonal = coupling(padded(cond_ext), shift_ext)
    first = schwarz_apply(source, weights, diagonal)
    cond_near = cond_ext[:, OV - 1 : OV + rows_here + 1, OV - 1 : OV + cols_here + 1]
    near_weights, near_diag = coupling(jnp.pad(cond_near, ((1, 1), (0, 0), (0, 0))), shift_term)
    beside_all = extended_2(first, (("aisle", 2), ("row", 1)), 1)
    near_row = row_place * rows_here - 1 + lax.iota(jnp.int32, rows_here + 2)
    near_out = ((near_row < 0) | (near_row >= rows_here * row_count))[None, :, None]
    beside_all = jnp.where(near_out, 0.0, beside_all)
    remain = source - operate(
        jnp.pad(beside_all, ((1, 1), (0, 0), (0, 0))), near_weights, near_diag
    )
    return first + schwarz_apply(remain, weights, diagonal)


def solution(mesh):
    return jax.shard_map(
        body,
        mesh=mesh,
        in_specs=(P(None, "row", "aisle"), P(None, "row", "aisle"), P(None, "row", "aisle")),
        out_specs=P(None, "row", "aisle"),
        check_vma=False,
    )
```

profile of v0, /device:TPU:64, one launch (start us, length us, event | category | flops | bytes accessed | tf_op | source)
XLA Modules:
  0.0 129.7 jit_solution(9654176097834466642)
XLA Ops:
  1.0 1.9 %collective-permute-start = (f32[2,8,16,2]{3,2,1,0:T(8,128)S(1)}, f32[2,8,16,2]{3,2,1,0:T(8,128)S(1)}, u32[]{:S(2)}, u32[]{:S(2)}) collective-permute-start(f32[2,8,16,2]{3,2,1,0:T(8,128)S(1)} %get-tuple-element.45), channel_id=1, source_target_pairs={{0,32},{32,64},{64,96},{96,128},{128,160},{160,192},{192,224},{224... | collective-permute-start | bytes 6152 | tf_op jit(solution)/shard_map/ppermute | solution.py:32
  2.9 16.3 %collective-permute-start.1 = (f32[2,8,16,2]{3,2,1,0:T(8,128)S(1)}, f32[2,8,16,2]{3,2,1,0:T(8,128)S(1)}, u32[]{:S(2)}, u32[]{:S(2)}) collective-permute-start(f32[2,8,16,2]{3,2,1,0:T(8,128)S(1)} %get-tuple-element.46), channel_id=1, source_target_pairs={{32,0},{64,32},{96,64},{128,96},{160,128},{192,160},{224,192},{256... | collective-permute-start | bytes 6152 | tf_op jit(solution)/shard_map/ppermute | solution.py:35
  19.9 1.8 %collective-permute-done.1 = f32[2,8,16,2]{3,2,1,0:T(8,128)S(1)} collective-permute-done((f32[2,8,16,2]{3,2,1,0:T(8,128)S(1)}, f32[2,8,16,2]{3,2,1,0:T(8,128)S(1)}, u32[]{:S(2)}, u32[]{:S(2)}) %collective-permute-start.1) | collective-permute-done | bytes 2080 | tf_op jit(solution)/shard_map/ppermute | solution.py:35
  21.9 4.3 %collective-permute-start.2 = (f32[2,8,2,132]{3,2,1,0:T(2,128)S(1)}, f32[2,8,2,132]{3,2,1,0:T(2,128)S(1)}, u32[]{:S(2)}, u32[]{:S(2)}) collective-permute-start(f32[2,8,2,132]{3,2,1,0:T(2,128)S(1)} %get-tuple-element.33), channel_id=1, source_target_pairs={{0,1},{1,2},{2,3},{3,4},{4,5},{5,6},{6,7},{7,8},{8,9},{9,10},{10,1... | collective-permute-start | bytes 50696 | tf_op jit(solution)/shard_map/ppermute | solution.py:32
  26.2 5.5 %collective-permute-start.3 = (f32[2,8,2,132]{3,2,1,0:T(2,128)S(1)}, f32[2,8,2,132]{3,2,1,0:T(2,128)S(1)}, u32[]{:S(2)}, u32[]{:S(2)}) collective-permute-start(f32[2,8,2,132]{3,2,1,0:T(2,128)S(1)} %get-tuple-element.34), channel_id=1, source_target_pairs={{1,0},{2,1},{3,2},{4,3},{5,4},{6,5},{7,6},{8,7},{9,8},{10,9},{11,1... | collective-permute-start | bytes 50696 | tf_op jit(solution)/shard_map/ppermute | solution.py:35
  36.5 5.4 %collective-permute-start.4 = (f32[8,20,2]{2,1,0:T(8,128)S(1)}, f32[8,20,2]{2,1,0:T(8,128)S(1)}, u32[]{:S(2)}, u32[]{:S(2)}) collective-permute-start(f32[8,20,2]{2,1,0:T(8,128)S(1)} %slice.541), channel_id=1, source_target_pairs={{992,0},{0,32},{32,64},{64,96},{96,128},{128,160},{160,192},{192,2... | collective-permute-start | bytes 3848 | tf_op jit(solution)/shard_map/ppermute | solution.py:17
  41.9 7.9 %collective-permute-done.4 = f32[8,20,2]{2,1,0:T(8,128)S(1)} collective-permute-done((f32[8,20,2]{2,1,0:T(8,128)S(1)}, f32[8,20,2]{2,1,0:T(8,128)S(1)}, u32[]{:S(2)}, u32[]{:S(2)}) %collective-permute-start.4) | collective-permute-done | bytes 1312 | tf_op jit(solution)/shard_map/ppermute | solution.py:17
  49.9 1.9 %collective-permute-start.5 = (f32[8,20,2]{2,1,0:T(8,128)S(1)}, f32[8,20,2]{2,1,0:T(8,128)S(1)}, u32[]{:S(2)}, u32[]{:S(2)}) collective-permute-start(f32[8,20,2]{2,1,0:T(8,128)S(1)} %get-tuple-element.44), channel_id=1, source_target_pairs={{32,0},{64,32},{96,64},{128,96},{160,128},{192,160},{224,192},{256... | collective-permute-start | bytes 3848 | tf_op jit(solution)/shard_map/ppermute | solution.py:17
  51.9 2.1 %collective-permute-done.5 = f32[8,20,2]{2,1,0:T(8,128)S(1)} collective-permute-done((f32[8,20,2]{2,1,0:T(8,128)S(1)}, f32[8,20,2]{2,1,0:T(8,128)S(1)}, u32[]{:S(2)}, u32[]{:S(2)}) %collective-permute-start.5) | collective-permute-done | bytes 1312 | tf_op jit(solution)/shard_map/ppermute | solution.py:17
  54.1 2.5 %collective-permute-start.6 = (f32[8,2,128]{2,1,0:T(2,128)S(1)}, f32[8,2,128]{2,1,0:T(2,128)S(1)}, u32[]{:S(2)}, u32[]{:S(2)}) collective-permute-start(f32[8,2,128]{2,1,0:T(2,128)S(1)} %pad_maximum_fusion.17), channel_id=1, source_target_pairs={{0,1},{1,2},{2,3},{3,4},{4,5},{5,6},{6,7},{7,8},{8,9},{9,10},{10,1... | collective-permute-start | bytes 24584 | tf_op jit(solution)/shard_map/ppermute | solution.py:23
  56.6 7.0 %collective-permute-done.6 = f32[8,2,128]{2,1,0:T(2,128)S(1)} collective-permute-done((f32[8,2,128]{2,1,0:T(2,128)S(1)}, f32[8,2,128]{2,1,0:T(2,128)S(1)}, u32[]{:S(2)}, u32[]{:S(2)}) %collective-permute-start.6) | collective-permute-done | bytes 8224 | tf_op jit(solution)/shard_map/ppermute | solution.py:23
  63.7 3.0 %collective-permute-start.7 = (f32[8,2,128]{2,1,0:T(2,128)S(1)}, f32[8,2,128]{2,1,0:T(2,128)S(1)}, u32[]{:S(2)}, u32[]{:S(2)}) collective-permute-start(f32[8,2,128]{2,1,0:T(2,128)S(1)} %get-tuple-element.38), channel_id=1, source_target_pairs={{1,0},{2,1},{3,2},{4,3},{5,4},{6,5},{7,6},{8,7},{9,8},{10,9},{11,1... | collective-permute-start | bytes 24584 | tf_op jit(solution)/shard_map/ppermute | solution.py:23
  66.9 2.4 %collective-permute-done.7 = f32[8,2,128]{2,1,0:T(2,128)S(1)} collective-permute-done((f32[8,2,128]{2,1,0:T(2,128)S(1)}, f32[8,2,128]{2,1,0:T(2,128)S(1)}, u32[]{:S(2)}, u32[]{:S(2)}) %collective-permute-start.7) | collective-permute-done | bytes 8224 | tf_op jit(solution)/shard_map/ppermute | solution.py:23
  69.4 2.1 %collective-permute-start.8 = (f32[8,16,1]{2,1,0:T(8,128)S(1)}, f32[8,16,1]{2,1,0:T(8,128)S(1)}, u32[]{:S(2)}, u32[]{:S(2)}) collective-permute-start(f32[8,16,1]{2,1,0:T(8,128)S(1)} %get-tuple-element.47), channel_id=1, source_target_pairs={{0,32},{32,64},{64,96},{96,128},{128,160},{160,192},{192,224},{224... | collective-permute-start | bytes 1544 | tf_op jit(solution)/shard_map/ppermute | solution.py:32
  71.6 9.4 %collective-permute-start.9 = (f32[8,16,1]{2,1,0:T(8,128)S(1)}, f32[8,16,1]{2,1,0:T(8,128)S(1)}, u32[]{:S(2)}, u32[]{:S(2)}) collective-permute-start(f32[8,16,1]{2,1,0:T(8,128)S(1)} %get-tuple-element.48), channel_id=1, source_target_pairs={{32,0},{64,32},{96,64},{128,96},{160,128},{192,160},{224,192},{256... | collective-permute-start | bytes 1544 | tf_op jit(solution)/shard_map/ppermute | solution.py:35
  83.1 1.9 %collective-permute-start.10 = (f32[8,1,130]{2,1,0:T(1,128)S(1)}, f32[8,1,130]{2,1,0:T(1,128)S(1)}, u32[]{:S(2)}, u32[]{:S(2)}) collective-permute-start(f32[8,1,130]{2,1,0:T(1,128)S(1)} %get-tuple-element.39), channel_id=1, source_target_pairs={{0,1},{1,2},{2,3},{3,4},{4,5},{5,6},{6,7},{7,8},{8,9},{9,10},{10,1... | collective-permute-start | bytes 12488 | tf_op jit(solution)/shard_map/ppermute | solution.py:32
  85.0 7.8 %collective-permute-start.11 = (f32[8,1,130]{2,1,0:T(1,128)S(1)}, f32[8,1,130]{2,1,0:T(1,128)S(1)}, u32[]{:S(2)}, u32[]{:S(2)}) collective-permute-start(f32[8,1,130]{2,1,0:T(1,128)S(1)} %get-tuple-element.40), channel_id=1, source_target_pairs={{1,0},{2,1},{3,2},{4,3},{5,4},{6,5},{7,6},{8,7},{9,8},{10,9},{11,1... | collective-permute-start | bytes 12488 | tf_op jit(solution)/shard_map/ppermute | solution.py:35
  96.7 1.9 %collective-permute-start.12 = (f32[8,20,2]{2,1,0:T(8,128)S(1)}, f32[8,20,2]{2,1,0:T(8,128)S(1)}, u32[]{:S(2)}, u32[]{:S(2)}) collective-permute-start(f32[8,20,2]{2,1,0:T(8,128)S(1)} %slice.560), channel_id=1, source_target_pairs={{992,0},{0,32},{32,64},{64,96},{96,128},{128,160},{160,192},{192,2... | collective-permute-start | bytes 3848 | tf_op jit(solution)/shard_map/ppermute | solution.py:17
  98.6 10.1 %collective-permute-done.12 = f32[8,20,2]{2,1,0:T(8,128)S(1)} collective-permute-done((f32[8,20,2]{2,1,0:T(8,128)S(1)}, f32[8,20,2]{2,1,0:T(8,128)S(1)}, u32[]{:S(2)}, u32[]{:S(2)}) %collective-permute-start.12) | collective-permute-done | bytes 1312 | tf_op jit(solution)/shard_map/ppermute | solution.py:17
  108.8 1.9 %collective-permute-start.13 = (f32[8,20,2]{2,1,0:T(8,128)S(1)}, f32[8,20,2]{2,1,0:T(8,128)S(1)}, u32[]{:S(2)}, u32[]{:S(2)}) collective-permute-start(f32[8,20,2]{2,1,0:T(8,128)S(1)} %get-tuple-element.42), channel_id=1, source_target_pairs={{32,0},{64,32},{96,64},{128,96},{160,128},{192,160},{224,192},{256... | collective-permute-start | bytes 3848 | tf_op jit(solution)/shard_map/ppermute | solution.py:17
  110.8 2.1 %collective-permute-done.13 = f32[8,20,2]{2,1,0:T(8,128)S(1)} collective-permute-done((f32[8,20,2]{2,1,0:T(8,128)S(1)}, f32[8,20,2]{2,1,0:T(8,128)S(1)}, u32[]{:S(2)}, u32[]{:S(2)}) %collective-permute-start.13) | collective-permute-done | bytes 1312 | tf_op jit(solution)/shard_map/ppermute | solution.py:17
  113.1 1.9 %collective-permute-start.14 = (f32[8,2,128]{2,1,0:T(2,128)S(1)}, f32[8,2,128]{2,1,0:T(2,128)S(1)}, u32[]{:S(2)}, u32[]{:S(2)}) collective-permute-start(f32[8,2,128]{2,1,0:T(2,128)S(1)} %pad_maximum_fusion.10), channel_id=1, source_target_pairs={{0,1},{1,2},{2,3},{3,4},{4,5},{5,6},{6,7},{7,8},{8,9},{9,10},{10,1... | collective-permute-start | bytes 24584 | tf_op jit(solution)/shard_map/ppermute | solution.py:23
  115.0 8.3 %collective-permute-done.14 = f32[8,2,128]{2,1,0:T(2,128)S(1)} collective-permute-done((f32[8,2,128]{2,1,0:T(2,128)S(1)}, f32[8,2,128]{2,1,0:T(2,128)S(1)}, u32[]{:S(2)}, u32[]{:S(2)}) %collective-permute-start.14) | collective-permute-done | bytes 8224 | tf_op jit(solution)/shard_map/ppermute | solution.py:23
  123.4 3.9 %collective-permute-start.15 = (f32[8,2,128]{2,1,0:T(2,128)S(1)}, f32[8,2,128]{2,1,0:T(2,128)S(1)}, u32[]{:S(2)}, u32[]{:S(2)}) collective-permute-start(f32[8,2,128]{2,1,0:T(2,128)S(1)} %get-tuple-element.36), channel_id=1, source_target_pairs={{1,0},{2,1},{3,2},{4,3},{5,4},{6,5},{7,6},{8,7},{9,8},{10,9},{11,1... | collective-permute-start | bytes 24584 | tf_op jit(solution)/shard_map/ppermute | solution.py:23
  (60 shorter events, 15.9 us)
Async XLA Ops:
  0.0 0.9 copy-start.1
  1.0 18.9 %collective-permute-start = (f32[2,8,16,2]{3,2,1,0:T(8,128)S(1)}, f32[2,8,16,2]{3,2,1,0:T(8,128)S(1)}, u32[]{:S(2)}, u32[]{:S(2)}) collective-permute-start(f32[2,8,16,2]{3,2,1,0:T(8,128)S(1)} %get-tuple-element.45), channel_id=1, source_target_pairs={{0,32},{32,64},{64,96},{96,128},{128,160},{160,192},{192,224},{224... | collective-permute-start | bytes 6152 | tf_op jit(solution)/shard_map/ppermute | solution.py:32
  2.9 18.8 %collective-permute-start.1 = (f32[2,8,16,2]{3,2,1,0:T(8,128)S(1)}, f32[2,8,16,2]{3,2,1,0:T(8,128)S(1)}, u32[]{:S(2)}, u32[]{:S(2)}) collective-permute-start(f32[2,8,16,2]{3,2,1,0:T(8,128)S(1)} %get-tuple-element.46), channel_id=1, source_target_pairs={{32,0},{64,32},{96,64},{128,96},{160,128},{192,160},{224,192},{256... | collective-permute-start | bytes 6152 | tf_op jit(solution)/shard_map/ppermute | solution.py:35
  21.9 9.8 %collective-permute-start.2 = (f32[2,8,2,132]{3,2,1,0:T(2,128)S(1)}, f32[2,8,2,132]{3,2,1,0:T(2,128)S(1)}, u32[]{:S(2)}, u32[]{:S(2)}) collective-permute-start(f32[2,8,2,132]{3,2,1,0:T(2,128)S(1)} %get-tuple-element.33), channel_id=1, source_target_pairs={{0,1},{1,2},{2,3},{3,4},{4,5},{5,6},{6,7},{7,8},{8,9},{9,10},{10,1... | collective-permute-start | bytes 50696 | tf_op jit(solution)/shard_map/ppermute | solution.py:32
  26.2 7.0 %collective-permute-start.3 = (f32[2,8,2,132]{3,2,1,0:T(2,128)S(1)}, f32[2,8,2,132]{3,2,1,0:T(2,128)S(1)}, u32[]{:S(2)}, u32[]{:S(2)}) collective-permute-start(f32[2,8,2,132]{3,2,1,0:T(2,128)S(1)} %get-tuple-element.34), channel_id=1, source_target_pairs={{1,0},{2,1},{3,2},{4,3},{5,4},{6,5},{7,6},{8,7},{9,8},{10,9},{11,1... | collective-permute-start | bytes 50696 | tf_op jit(solution)/shard_map/ppermute | solution.py:35
  33.5 0.8 copy-start
  36.5 13.3 %collective-permute-start.4 = (f32[8,20,2]{2,1,0:T(8,128)S(1)}, f32[8,20,2]{2,1,0:T(8,128)S(1)}, u32[]{:S(2)}, u32[]{:S(2)}) collective-permute-start(f32[8,20,2]{2,1,0:T(8,128)S(1)} %slice.541), channel_id=1, source_target_pairs={{992,0},{0,32},{32,64},{64,96},{96,128},{128,160},{160,192},{192,2... | collective-permute-start | bytes 3848 | tf_op jit(solution)/shard_map/ppermute | solution.py:17
  49.9 4.1 %collective-permute-start.5 = (f32[8,20,2]{2,1,0:T(8,128)S(1)}, f32[8,20,2]{2,1,0:T(8,128)S(1)}, u32[]{:S(2)}, u32[]{:S(2)}) collective-permute-start(f32[8,20,2]{2,1,0:T(8,128)S(1)} %get-tuple-element.44), channel_id=1, source_target_pairs={{32,0},{64,32},{96,64},{128,96},{160,128},{192,160},{224,192},{256... | collective-permute-start | bytes 3848 | tf_op jit(solution)/shard_map/ppermute | solution.py:17
  54.1 9.5 %collective-permute-start.6 = (f32[8,2,128]{2,1,0:T(2,128)S(1)}, f32[8,2,128]{2,1,0:T(2,128)S(1)}, u32[]{:S(2)}, u32[]{:S(2)}) collective-permute-start(f32[8,2,128]{2,1,0:T(2,128)S(1)} %pad_maximum_fusion.17), channel_id=1, source_target_pairs={{0,1},{1,2},{2,3},{3,4},{4,5},{5,6},{6,7},{7,8},{8,9},{9,10},{10,1... | collective-permute-start | bytes 24584 | tf_op jit(solution)/shard_map/ppermute | solution.py:23
  63.7 5.5 %collective-permute-start.7 = (f32[8,2,128]{2,1,0:T(2,128)S(1)}, f32[8,2,128]{2,1,0:T(2,128)S(1)}, u32[]{:S(2)}, u32[]{:S(2)}) collective-permute-start(f32[8,2,128]{2,1,0:T(2,128)S(1)} %get-tuple-element.38), channel_id=1, source_target_pairs={{1,0},{2,1},{3,2},{4,3},{5,4},{6,5},{7,6},{8,7},{9,8},{10,9},{11,1... | collective-permute-start | bytes 24584 | tf_op jit(solution)/shard_map/ppermute | solution.py:23
  69.4 12.2 %collective-permute-start.8 = (f32[8,16,1]{2,1,0:T(8,128)S(1)}, f32[8,16,1]{2,1,0:T(8,128)S(1)}, u32[]{:S(2)}, u32[]{:S(2)}) collective-permute-start(f32[8,16,1]{2,1,0:T(8,128)S(1)} %get-tuple-element.47), channel_id=1, source_target_pairs={{0,32},{32,64},{64,96},{96,128},{128,160},{160,192},{192,224},{224... | collective-permute-start | bytes 1544 | tf_op jit(solution)/shard_map/ppermute | solution.py:32
  71.6 11.3 %collective-permute-start.9 = (f32[8,16,1]{2,1,0:T(8,128)S(1)}, f32[8,16,1]{2,1,0:T(8,128)S(1)}, u32[]{:S(2)}, u32[]{:S(2)}) collective-permute-start(f32[8,16,1]{2,1,0:T(8,128)S(1)} %get-tuple-element.48), channel_id=1, source_target_pairs={{32,0},{64,32},{96,64},{128,96},{160,128},{192,160},{224,192},{256... | collective-permute-start | bytes 1544 | tf_op jit(solution)/shard_map/ppermute | solution.py:35
  83.1 9.9 %collective-permute-start.10 = (f32[8,1,130]{2,1,0:T(1,128)S(1)}, f32[8,1,130]{2,1,0:T(1,128)S(1)}, u32[]{:S(2)}, u32[]{:S(2)}) collective-permute-start(f32[8,1,130]{2,1,0:T(1,128)S(1)} %get-tuple-element.39), channel_id=1, source_target_pairs={{0,1},{1,2},{2,3},{3,4},{4,5},{5,6},{6,7},{7,8},{8,9},{9,10},{10,1... | collective-permute-start | bytes 12488 | tf_op jit(solution)/shard_map/ppermute | solution.py:32
  85.0 9.2 %collective-permute-start.11 = (f32[8,1,130]{2,1,0:T(1,128)S(1)}, f32[8,1,130]{2,1,0:T(1,128)S(1)}, u32[]{:S(2)}, u32[]{:S(2)}) collective-permute-start(f32[8,1,130]{2,1,0:T(1,128)S(1)} %get-tuple-element.40), channel_id=1, source_target_pairs={{1,0},{2,1},{3,2},{4,3},{5,4},{6,5},{7,6},{8,7},{9,8},{10,9},{11,1... | collective-permute-start | bytes 12488 | tf_op jit(solution)/shard_map/ppermute | solution.py:35
  93.0 1.4 %copy-start.2 = (s32[8,16,128]{2,1,0:T(8,128)S(1)}, s32[8,16,128]{2,1,0:T(8,128)}, u32[]{:S(2)}) copy-start(s32[8,16,128]{2,1,0:T(8,128)} %param.5) | copy-start | bytes 196612
  96.7 12.0 %collective-permute-start.12 = (f32[8,20,2]{2,1,0:T(8,128)S(1)}, f32[8,20,2]{2,1,0:T(8,128)S(1)}, u32[]{:S(2)}, u32[]{:S(2)}) collective-permute-start(f32[8,20,2]{2,1,0:T(8,128)S(1)} %slice.560), channel_id=1, source_target_pairs={{992,0},{0,32},{32,64},{64,96},{96,128},{128,160},{160,192},{192,2... | collective-permute-start | bytes 3848 | tf_op jit(solution)/shard_map/ppermute | solution.py:17
  108.8 4.1 %collective-permute-start.13 = (f32[8,20,2]{2,1,0:T(8,128)S(1)}, f32[8,20,2]{2,1,0:T(8,128)S(1)}, u32[]{:S(2)}, u32[]{:S(2)}) collective-permute-start(f32[8,20,2]{2,1,0:T(8,128)S(1)} %get-tuple-element.42), channel_id=1, source_target_pairs={{32,0},{64,32},{96,64},{128,96},{160,128},{192,160},{224,192},{256... | collective-permute-start | bytes 3848 | tf_op jit(solution)/shard_map/ppermute | solution.py:17
  113.1 10.3 %collective-permute-start.14 = (f32[8,2,128]{2,1,0:T(2,128)S(1)}, f32[8,2,128]{2,1,0:T(2,128)S(1)}, u32[]{:S(2)}, u32[]{:S(2)}) collective-permute-start(f32[8,2,128]{2,1,0:T(2,128)S(1)} %pad_maximum_fusion.10), channel_id=1, source_target_pairs={{0,1},{1,2},{2,3},{3,4},{4,5},{5,6},{6,7},{7,8},{8,9},{9,10},{10,1... | collective-permute-start | bytes 24584 | tf_op jit(solution)/shard_map/ppermute | solution.py:23
  123.4 5.5 %collective-permute-start.15 = (f32[8,2,128]{2,1,0:T(2,128)S(1)}, f32[8,2,128]{2,1,0:T(2,128)S(1)}, u32[]{:S(2)}, u32[]{:S(2)}) collective-permute-start(f32[8,2,128]{2,1,0:T(2,128)S(1)} %get-tuple-element.36), channel_id=1, source_target_pairs={{1,0},{2,1},{3,2},{4,3},{5,4},{6,5},{7,6},{8,7},{9,8},{10,9},{11,1... | collective-permute-start | bytes 24584 | tf_op jit(solution)/shard_map/ppermute | solution.py:23
where the time goes:
time: 130 us
  starting transfers between devices  71.8 us (55%)
  waiting for transfers between devices  48.5 us (37%)
  other arithmetic  7.77 us (6%)
    ppermute x4, starting transfers between devices, extended_2(): lax.ppermute(lax.slice_in_dim(block, 0, width, axis=dim), axis, backward)  39 us
    ppermute x4, waiting for transfers between devices, shifted(): return lax.ppermute(block, axis, route)  22.2 us
    ppermute x4, waiting for transfers between devices, from_behind(): return lax.ppermute(shard, axis, pairs)  19.1 us
    ppermute x4, starting transfers between devices, from_behind(): return lax.ppermute(shard, axis, pairs)  11.3 us
    ppermute x4, starting transfers between devices, shifted(): return lax.ppermute(block, axis, route)  11.1 us
    ppermute x4, starting transfers between devices, extended_2(): lax.ppermute(lax.slice_in_dim(block, block.shape[dim] - width, None, axis...  10.3 us
    ppermute x4, waiting for transfers between devices, extended_2(): lax.ppermute(lax.slice_in_dim(block, 0, width, axis=dim), axis, backward)  5.79 us
    add x12, other arithmetic, smooth_local(): estimate = estimate + update  3.61 us
  transfers between devices with their start and end apart: 16, of which 14 were waited for; matrix products, arithmetic and copies ran while one was open for 0% of the time, Pallas kernels for 0%

commit v1 on v0

v1 whole, which is shorter than its diff:
```python
import functools
import math

import jax
import jax.numpy as jnp
from jax import lax
from jax.experimental import pallas as pl
from jax.experimental.pallas import tpu as pltpu
from jax.sharding import PartitionSpec as P

MESH = pl.DeviceIdType.MESH
NZ, ROWS, COLS = 8, 16, 128

MIDDLE, SPREAD, STEPS = 1.1, 0.9, 7
ORDER = (4, 1, 7, 3, 5, 2, 6)
TAUS = tuple(1.0 / (MIDDLE + SPREAD * math.cos(math.pi * (2 * k - 1) / (2 * STEPS))) for k in ORDER)

FIRST_ROW = (-13, -2, 14)
LENGTH = (15, 20, 15)
SKEW = (40, 0, 88)
BASE = (0, 15, 35)
SIDE = 50
TILES = 70
K_ROWS = (range(-14, 2), range(-2, 18), range(14, 30))


def roll(x, by):
    by = by % COLS
    return x if by == 0 else pltpu.roll(x, by, 1)


def vroll(x, by):
    return pltpu.roll(x, by % NZ, 0)


def kernel(src_hbm, cond_hbm, solid_hbm, out_ref,
           own_src, own_cond, own_solid, to_side, ns_src, ns_cond, ns_solid, from_side,
           half, half_side, wgt, rhs, est, first,
           load_sem, send_sem, recv_sem):
    n_a, n_r = lax.axis_size("aisle"), lax.axis_size("row")
    a, r = lax.axis_index("aisle"), lax.axis_index("row")
    has_n, has_s = r > 0, r < n_r - 1

    def device(da, dr):
        return {"aisle": lax.rem(a + (da + n_a), n_a), "row": lax.rem(r + (dr + n_r), n_r)}

    loads = [
        pltpu.make_async_copy(h, v, load_sem.at[i])
        for i, (h, v) in enumerate(((cond_hbm, own_cond), (solid_hbm, own_solid), (src_hbm, own_src)))
    ]
    for c in loads:
        c.start()

    around = [(da, dr) for da in (-1, 0, 1) for dr in (-1, 0, 1) if (da, dr) != (0, 0)]
    barrier = pltpu.get_barrier_semaphore()
    for da, dr in around:
        pl.semaphore_signal(barrier, inc=1, device_id=device(da, dr), device_id_type=MESH)

    lane = lax.broadcasted_iota(jnp.int32, (NZ, COLS), 1)
    level = lax.broadcasted_iota(jnp.int32, (NZ, COLS), 0)
    rel = [lax.rem(lane + (COLS - s), COLS) for s in SKEW]
    mine = [(q < 18) | (q >= 110) for q in rel]
    relx = jnp.where(mine[0], rel[0], jnp.where(mine[2], rel[2], rel[1]))
    band = jnp.where(mine[0], 0, jnp.where(mine[2], 2, 1))
    code = band * COLS + relx
    zero = jnp.zeros((NZ, COLS), jnp.float32)
    one = jnp.ones((NZ, COLS), jnp.float32)

    def own_row(kind, row):
        rows = pl.ds(row, NZ, stride=ROWS)
        if kind == 0:
            return own_cond[rows, :]
        if kind == 1:
            return 0.05 + 20.0 * own_solid[rows, :].astype(jnp.float32)
        return own_src[rows, :]

    for c in loads:
        c.wait()
    slot = lax.div(lane, 16)
    for kind in range(3):
        for half_of in range(2):
            west, east = zero, zero
            for s in range(8):
                v = own_row(kind, half_of * 8 + s)
                here = slot == s
                west = jnp.where(here, roll(v, 16 * s), west)
                east = jnp.where(here, roll(v, 16 * s + 14), east)
            to_side[0, kind * 2 + half_of] = west
            to_side[1, kind * 2 + half_of] = east

    pl.semaphore_wait(barrier, len(around))

    copies = []

    def send(source, target, n, da, dr):
        c = pltpu.make_async_remote_copy(
            src_ref=source, dst_ref=target, send_sem=send_sem.at[n], recv_sem=recv_sem.at[n],
            device_id=device(da, dr), device_id_type=MESH)
        c.start()
        copies.append(c)

    n = 0
    for dr in (-1, 1, 0):
        for da in (-1, 1):
            send(to_side.at[0 if da < 0 else 1], from_side.at[(3 if da < 0 else 0) + 1 - dr], n, da, dr)
            n += 1
    for dr in (-1, 1):
        where = 1 if dr < 0 else 0
        for source, target in ((cond_hbm, ns_cond), (solid_hbm, ns_solid), (src_hbm, ns_src)):
            send(source, target.at[where], n, 0, dr)
            n += 1
    for c in copies:
        c.wait_recv()

    fill = (zero, one, zero)

    def main_row(kind, row):
        if 0 <= row < ROWS:
            return own_row(kind, row)
        w, exists = (0, has_n) if row < 0 else (1, has_s)
        rows = pl.ds(row % ROWS, NZ, stride=ROWS)
        if kind == 0:
            v = ns_cond[w, rows, :]
        elif kind == 1:
            v = 0.05 + 20.0 * ns_solid[w, rows, :].astype(jnp.float32)
        else:
            v = ns_src[w, rows, :]
        return jnp.where(exists, v, fill[kind])

    def strips(kind, row):
        which = 0 if row < 0 else (1 if row < ROWS else 2)
        q = row % ROWS
        return from_side[which, kind * 2 + q // 8], from_side[3 + which, kind * 2 + q // 8], 16 * (q % 8)

    def side_tile(kind, j, mains):
        tile = fill[kind]
        for g in range(3):
            row = FIRST_ROW[g] + j
            if row not in K_ROWS[g] or (kind and not 0 <= j < LENGTH[g]):
                continue
            in_core = (row < 0, 0 <= row < ROWS, row >= ROWS)[g]
            if kind == 2 and not in_core:
                continue
            at = g * COLS
            w, e, off = strips(kind, row)
            part = jnp.where(relx < 64, roll(e, 4 + SKEW[g] - off), roll(w, SKEW[g] - 18 - off))
            if kind == 2:
                keep = ((code >= at + 4) & (code < at + 18)) | ((code >= at + 110) & (code < at + 124))
                part = jnp.where(keep, part, 0.0)
            else:
                m = mains[g]
                own = jnp.where(relx < 64, roll(m, 4), roll(m, -4))
                part = jnp.where((relx < 4) | (relx >= 124), own, part)
            exists = has_n if row < 0 else (has_s if row >= ROWS else None)
            if exists is not None:
                part = jnp.where(exists, part, fill[kind])
            tile = jnp.where((band == g) & mine_any, part, tile)
        if kind != 2:
            tile = jnp.where(relx < 2, roll(tile, -4), jnp.where(relx >= 126, roll(tile, 4), tile))
            tile = jnp.where(mine_any, tile, fill[kind])
        return tile

    mine_any = mine[0] | mine[1] | mine[2]

    def hidx(g, j):
        return (0, 16, 36)[g] + j + (1 if g == 0 else 0)

    for j in range(-1, 20):
        mains = {}
        for g in range(3):
            row = FIRST_ROW[g] + j
            if row in K_ROWS[g]:
                mains[g] = roll(main_row(0, row), SKEW[g])
                half[hidx(g, j)] = 0.5 * mains[g]
        half_side[j + 1] = 0.5 * side_tile(0, j, mains)

    def around_cols(mains, side):
        sp, sm = roll(side, -1), roll(side, 1)
        out, plus, minus = {}, sp, sm
        for g, m in mains.items():
            mp, mm = roll(m, -1), roll(m, 1)
            out[g] = (jnp.where(rel[g] == 127, sp, mp), jnp.where(rel[g] == 0, sm, mm))
            plus = jnp.where(code == g * COLS + 127, mp, plus)
            minus = jnp.where(code == g * COLS, mm, minus)
        out[3] = (plus, minus)
        return out

    top, bottom = level == NZ - 1, level == 0
    no_plus = (relx == 1) | (relx == 125)
    no_minus = (relx == 2) | (relx == 126)
    live = mine_any & ((relx < 17) | (relx > 110))

    def weights(at, h, s, up, down, plus, minus, side, alive):
        vp = h + jnp.where(top, 0.0, vroll(h, -1))
        vm = h + jnp.where(bottom, 0.0, vroll(h, 1))
        rp = h + down
        rm = h + up
        cp = h + (jnp.where(no_plus, 0.0, plus) if side else plus)
        cm = h + (jnp.where(no_minus, 0.0, minus) if side else minus)
        inverse = 1.0 / ((((((s + vp) + vm) + rp) + rm) + cp) + cm)
        if side:
            inverse = jnp.where(alive, inverse, 0.0)
        wgt[0, at] = jnp.where(top, 0.0, inverse * vp)
        wgt[1, at] = jnp.where(bottom, 0.0, inverse * vm)
        wgt[2, at] = inverse * rp
        wgt[3, at] = inverse * rm
        cp, cm = inverse * cp, inverse * cm
        wgt[4, at] = jnp.where(no_plus, 0.0, cp) if side else cp
        wgt[5, at] = jnp.where(no_minus, 0.0, cm) if side else cm
        return inverse

    tau0 = TAUS[0]
    for j in range(20):
        bands = [g for g in range(3) if j < LENGTH[g]]
        mains = {g: half[hidx(g, j)] for g in bands}
        side = half_side[j + 1]
        cols = around_cols(mains, side)
        shifts = {}
        for g in bands:
            row = FIRST_ROW[g] + j
            shifts[g] = roll(main_row(1, row), SKEW[g])
            up = half[hidx(g, j - 1)] if row - 1 in K_ROWS[g] else zero
            down = half[hidx(g, j + 1)] if row + 1 in K_ROWS[g] else zero
            inverse = weights(BASE[g] + j, mains[g], shifts[g], up, down, *cols[g], False, None)
            if (row < 0, 0 <= row < ROWS, row >= ROWS)[g]:
                b = inverse * roll(main_row(2, row), SKEW[g])
            else:
                b = zero
            rhs[BASE[g] + j] = b
            est[BASE[g] + j] = tau0 * b
        alive = live
        if len(bands) == 1:
            alive = live & (band == 1)
        up = half_side[j]
        if j == 0:
            up = jnp.where(band == 0, up, 0.0)
        down = half_side[j + 2] if j < 19 else zero
        inverse = weights(SIDE + j, side, side_tile(1, j, shifts), up, down, *cols[3], True, alive)
        b = inverse * side_tile(2, j, None)
        rhs[SIDE + j] = b
        est[SIDE + j] = tau0 * b

    def stencil(ref, b, spans, emit):
        def load(g, j):
            if g == 3:
                return ref[SIDE + j] if 0 <= j < 20 else None
            return ref[BASE[g] + j] if j in spans[g] else None

        old = {(g, j): load(g, j) for g in range(4) for j in (-1, 0)}
        for j in range(20):
            for g in range(4):
                old[g, j + 1] = load(g, j + 1)
            mains = {g: old[g, j] for g in range(3) if old[g, j] is not None}
            cols = around_cols(mains, old[3, j])
            for g in (*mains, 3):
                at = (SIDE if g == 3 else BASE[g]) + j
                x = old[g, j]
                plus, minus = cols[g]
                total = b[at] + wgt[0, at] * vroll(x, -1)
                other = wgt[1, at] * vroll(x, 1)
                if old[g, j + 1] is not None:
                    total = total + wgt[2, at] * old[g, j + 1]
                if old[g, j - 1] is not None:
                    other = other + wgt[3, at] * old[g, j - 1]
                total = total + wgt[4, at] * plus
                other = other + wgt[5, at] * minus
                emit(at, g, j, total + other, x)

    def solve(spans):
        def sweep(t, carry):
            tau = jnp.float32(TAUS[STEPS - 1])
            for i in range(STEPS - 2, 0, -1):
                tau = jnp.where(t == i, jnp.float32(TAUS[i]), tau)

            def emit(at, g, j, total, x):
                est[at] = x + tau * (total - x)

            stencil(est, rhs, spans, emit)
            return carry

        lax.fori_loop(1, STEPS, sweep, 0)

    full = [range(n) for n in LENGTH]
    solve(full)

    def gather_rows(g, j):
        v = est[BASE[g] + j]
        if g == 1 and j < 4:
            v = v + roll(est[BASE[0] + j + 11], -SKEW[0])
        if g == 1 and j >= 16:
            v = v + roll(est[BASE[2] + j - 16], -SKEW[2])
        if g == 0 and j >= 11:
            v = v + roll(est[BASE[1] + j - 11], SKEW[0])
        if g == 2 and j < 4:
            v = v + roll(est[BASE[1] + j + 16], SKEW[2])
        return v

    def gather_rows_side(j):
        v = est[SIDE + j]
        if j < 4:
            v = v + jnp.where(band == 1, roll(est[SIDE + j + 11], -SKEW[0]), 0.0)
            v = v + jnp.where(band == 2, roll(est[SIDE + j + 16], SKEW[2]), 0.0)
        if j >= 16:
            v = v + jnp.where(band == 1, roll(est[SIDE + j - 16], -SKEW[2]), 0.0)
        if 11 <= j < 15:
            v = v + jnp.where(band == 0, roll(est[SIDE + j - 11], SKEW[0]), 0.0)
        return jnp.where(mine_any, v, 0.0)

    near = [range(6, 15), range(0, 20), range(0, 9)]
    from_minus = (relx == 126) | (relx == 127) | (relx == 4) | (relx == 5)
    from_plus = (relx == 122) | (relx == 123) | (relx == 0) | (relx == 1)
    from_main_minus = (relx == 2) | (relx == 3)
    from_main_plus = (relx == 124) | (relx == 125)
    for j in range(20):
        side = gather_rows_side(j)
        s4, s_4 = roll(side, 4), roll(side, -4)
        add = jnp.where(from_minus, s4, jnp.where(from_plus, s_4, 0.0))
        exists = has_n if j < 2 else (has_s if j >= 18 else None)
        for g in range(3):
            if j not in near[g]:
                continue
            m = gather_rows(g, j)
            f = m + jnp.where(rel[g] < 2, s4, jnp.where(rel[g] >= 126, s_4, 0.0))
            cross = jnp.where(from_main_minus, roll(m, 4), jnp.where(from_main_plus, roll(m, -4), add))
            add = jnp.where(band == g, cross, add)
            if g == 1 and exists is not None:
                f = jnp.where(exists, f, 0.0)
            first[BASE[g] + j] = f
        f = side + add
        if exists is not None:
            f = jnp.where((band != 1) | exists, f, 0.0)
        first[SIDE + j] = f

    core_lane = ((relx >= 4) & (relx < 17)) | ((relx > 110) & (relx < 124))

    def emit_rhs(at, g, j, total, x):
        b = total - x
        if g == 3:
            keep = core_lane & mine_any
            use = []
            if 7 <= j <= 12:
                use.append((band == 0) & has_n)
            if 2 <= j <= 17:
                use.append(band == 1)
            if 2 <= j <= 7:
                use.append((band == 2) & has_s)
            if not use:
                b = zero
            else:
                any_use = use[0]
                for u in use[1:]:
                    any_use = any_use | u
                b = jnp.where(keep & any_use, b, 0.0)
        elif g == 0:
            b = jnp.where(has_n, b, 0.0) if 7 <= j <= 12 else zero
        elif g == 2:
            b = jnp.where(has_s, b, 0.0) if 2 <= j <= 7 else zero
        elif not 2 <= j <= 17:
            b = zero
        rhs[at] = b
        est[at] = tau0 * b

    stencil(first, rhs, near, emit_rhs)

    solve([range(7, 15), range(0, 20), range(0, 8)])

    for j in range(2, 18):
        side = est[SIDE + j]
        if j < 4:
            side = side + roll(est[SIDE + j + 11], -SKEW[0])
        if j >= 16:
            side = side + roll(est[SIDE + j - 16], -SKEW[2])
        v = first[BASE[1] + j] + gather_rows(1, j)
        v = v + jnp.where(lane < 2, roll(side, 4), jnp.where(lane >= 126, roll(side, -4), 0.0))
        out_ref[pl.ds(j - 2, NZ, stride=ROWS), :] = v

    for c in copies:
        c.wait_send()


def body(source, conduct, solid):
    flat = (NZ * ROWS, COLS)
    f32, i32 = jnp.float32, jnp.int32
    tile = (NZ, COLS)
    out = pl.pallas_call(
        kernel,
        out_shape=jax.ShapeDtypeStruct(flat, f32),
        in_specs=[pl.BlockSpec(memory_space=pltpu.HBM)] * 3,
        out_specs=pl.BlockSpec(memory_space=pltpu.VMEM),
        scratch_shapes=[
            pltpu.VMEM(flat, f32), pltpu.VMEM(flat, f32), pltpu.VMEM(flat, i32),
            pltpu.VMEM((2, 6, *tile), f32),
            pltpu.VMEM((2, *flat), f32), pltpu.VMEM((2, *flat), f32), pltpu.VMEM((2, *flat), i32),
            pltpu.VMEM((6, 6, *tile), f32),
            pltpu.VMEM((52, *tile), f32), pltpu.VMEM((21, *tile), f32),
            pltpu.VMEM((6, TILES, *tile), f32),
            pltpu.VMEM((TILES, *tile), f32), pltpu.VMEM((TILES, *tile), f32), pltpu.VMEM((TILES, *tile), f32),
            pltpu.SemaphoreType.DMA((3,)), pltpu.SemaphoreType.DMA((12,)), pltpu.SemaphoreType.DMA((12,)),
        ],
        compiler_params=pltpu.CompilerParams(
            collective_id=0, has_side_effects=True, vmem_limit_bytes=16 * 1024 * 1024),
    )(*(pltpu.with_memory_space_constraint(x.reshape(flat), pltpu.HBM) for x in (source, conduct, solid)))
    return out.reshape(source.shape)


def solution(mesh):
    spec = P(None, "row", "aisle")
    return jax.shard_map(body, mesh=mesh, in_specs=(spec, spec, spec), out_specs=spec, check_vma=False)
```

time: 130 us -> 39.9 us (0.31)
  the two profiles are of different devices: /device:TPU:64 before, /device:TPU:1 now
where the time goes in v1:
time: 39.9 us; the launch traced here: 39.7 us
  Pallas kernels  39.1 us (98%)
  local copies, waits for them, and re-layouts  0.63 us (2%)
    pallas_call x1, Pallas kernels, body(): pl.pallas_call(kernel, out_shape=jax.ShapeDtypeStruct(flat, f32), in_spec...  39.1 us

profile of v1, /device:TPU:1, one launch (start us, length us, event | category | flops | bytes accessed | tf_op | source)
XLA Modules:
  0.0 39.7 jit_solution(13886304157840029257)
XLA Ops:
  0.0 39.1 %shard_map.37 = f32[128,128]{1,0:T(8,128)S(1)} custom-call(f32[128,128]{1,0:T(8,128)} %bitcast.5, f32[128,128]{1,0:T(8,128)} %bitcast.6, s32[128,128]{1,0:T(8,128)} %bitcast.7), custom_call_target="tpu_custom_call" | custom-call | tf_op jit(solution)/shard_map/pallas_call | solution.py:385
  39.1 0.6 %copy.5 = f32[8,16,128]{2,1,0:T(8,128)} copy(f32[8,16,128]{2,1,0:T(8,128)S(1)} %bitcast.4) | data formatting | bytes 131072

commit v2 on v1

--- a/solution.py
+++ b/solution.py
@@ -12,6 +12,7 @@
 NZ, ROWS, COLS = 8, 16, 128
 
 MIDDLE, SPREAD, STEPS = 1.1, 0.9, 7
+CHUNK = (4, 2, 4, 8, 2, 7)
 ORDER = (4, 1, 7, 3, 5, 2, 6)
 TAUS = tuple(1.0 / (MIDDLE + SPREAD * math.cos(math.pi * (2 * k - 1) / (2 * STEPS))) for k in ORDER)
 
@@ -36,7 +37,7 @@
 def kernel(src_hbm, cond_hbm, solid_hbm, out_ref,
            own_src, own_cond, own_solid, to_side, ns_src, ns_cond, ns_solid, from_side,
            half, half_side, wgt, rhs, est, first,
-           load_sem, send_sem, recv_sem):
+           load_sem, send_sem, recv_sem, ready_sem):
     n_a, n_r = lax.axis_size("aisle"), lax.axis_size("row")
     a, r = lax.axis_index("aisle"), lax.axis_index("row")
     has_n, has_s = r > 0, r < n_r - 1
@@ -51,10 +52,47 @@
     for c in loads:
         c.start()
 
-    around = [(da, dr) for da in (-1, 0, 1) for dr in (-1, 0, 1) if (da, dr) != (0, 0)]
+    def order(pos_a, pos_r):
+        plane = lax.rem(lax.div(pos_a, 2), 2) * 4 + lax.rem(pos_r, 4)
+        return jnp.where((pos_a == 0) & (pos_r == 0), 15, plane * 4 + lax.rem(pos_a, 2) * 2)
+
+    near_side = 1 - 2 * lax.rem(a, 2)
+    sides = {"own": 0, "near": near_side, "far": -near_side}
+    ways = [("own", 1), ("near", 0), ("near", 1), ("near", -1), ("own", -1), ("far", 0), ("far", 1), ("far", -1)]
+    place = {w: i for i, w in enumerate(ways)}
+
+    def order(pos_a, pos_r):
+        plane = lax.rem(lax.div(pos_a, 2), 2) * 4 + lax.rem(pos_r, 4)
+        return jnp.where((pos_a == 0) & (pos_r == 0), 15, plane * 4 + lax.rem(pos_a, 2) * 2)
+
+    here_at = order(a, r)
+    earlier, n_earlier = {}, 0
+    for side, dr in ways:
+        there = device(sides[side], dr)
+        earlier[side, dr] = order(there["aisle"], there["row"]) < here_at
+        n_earlier = n_earlier + earlier[side, dr].astype(jnp.int32)
     barrier = pltpu.get_barrier_semaphore()
-    for da, dr in around:
-        pl.semaphore_signal(barrier, inc=1, device_id=device(da, dr), device_id_type=MESH)
+    for w in ways:
+        @pl.when(jnp.logical_not(earlier[w]))
+        def _():
+            pl.semaphore_signal(barrier, inc=1, device_id=device(sides[w[0]], w[1]), device_id_type=MESH)
+
+    @pl.when(n_earlier > 0)
+    def _():
+        pl.semaphore_wait(barrier, n_earlier)
+
+    for w in ways:
+        @pl.when(earlier[w])
+        def _():
+            pl.semaphore_signal(ready_sem.at[place[w[0], -w[1]]], inc=1, device_id=device(sides[w[0]], w[1]), device_id_type=MESH)
+
+    def blocks(indices, size, do):
+        indices = list(indices)
+        for at in range(0, len(indices), size):
+            @pl.when(r >= 0)
+            def _():
+                for i in indices[at:at + size]:
+                    do(i)
 
     lane = lax.broadcasted_iota(jnp.int32, (NZ, COLS), 1)
     level = lax.broadcasted_iota(jnp.int32, (NZ, COLS), 0)
@@ -77,40 +115,50 @@
     for c in loads:
         c.wait()
     slot = lax.div(lane, 16)
-    for kind in range(3):
-        for half_of in range(2):
-            west, east = zero, zero
-            for s in range(8):
-                v = own_row(kind, half_of * 8 + s)
-                here = slot == s
-                west = jnp.where(here, roll(v, 16 * s), west)
-                east = jnp.where(here, roll(v, 16 * s + 14), east)
-            to_side[0, kind * 2 + half_of] = west
-            to_side[1, kind * 2 + half_of] = east
-
-    pl.semaphore_wait(barrier, len(around))
-
-    copies = []
-
-    def send(source, target, n, da, dr):
-        c = pltpu.make_async_remote_copy(
-            src_ref=source, dst_ref=target, send_sem=send_sem.at[n], recv_sem=recv_sem.at[n],
-            device_id=device(da, dr), device_id_type=MESH)
-        c.start()
-        copies.append(c)
-
-    n = 0
-    for dr in (-1, 1, 0):
-        for da in (-1, 1):
-            send(to_side.at[0 if da < 0 else 1], from_side.at[(3 if da < 0 else 0) + 1 - dr], n, da, dr)
+    def pack(i):
+        kind, half_of = divmod(i, 2)
+        west, east = zero, zero
+        for s in range(8):
+            v = own_row(kind, half_of * 8 + s)
+            here = slot == s
+            west = jnp.where(here, roll(v, 16 * s), west)
+            east = jnp.where(here, roll(v, 16 * s + 14), east)
+        to_side[0, i] = west
+        to_side[1, i] = east
+
+    blocks(range(6), CHUNK[4], pack)
+
+    copies, n = {}, 0
+    for side, dr in ways:
+        if side == "own":
+            w = 1 if dr < 0 else 0
+            pairs = [(cond_hbm, ns_cond.at[w]), (solid_hbm, ns_solid.at[w]), (src_hbm, ns_src.at[w])]
+        else:
+            east = lax.div(sides[side] + 1, 2)
+            pairs = [(to_side.at[east], from_side.at[3 * (1 - east) + 1 - dr])]
+        copies[side, dr] = []
+        for source, target in pairs:
+            copies[side, dr].append(pltpu.make_async_remote_copy(
+                src_ref=source, dst_ref=target, send_sem=send_sem.at[n], recv_sem=recv_sem.at[n],
+                device_id=device(sides[side], dr), device_id_type=MESH))
             n += 1
-    for dr in (-1, 1):
-        where = 1 if dr < 0 else 0
-        for source, target in ((cond_hbm, ns_cond), (solid_hbm, ns_solid), (src_hbm, ns_src)):
-            send(source, target.at[where], n, 0, dr)
-            n += 1
-    for c in copies:
-        c.wait_recv()
+    for w in ways[::-1]:
+        @pl.when(earlier[w])
+        def _():
+            for c in copies[w]:
+                c.start()
+    def send_later(which):
+        for w in which:
+            @pl.when(jnp.logical_not(earlier[w]))
+            def _():
+                pl.semaphore_wait(ready_sem.at[place[w]], 1)
+                for c in copies[w]:
+                    c.start()
+
+    send_later(ways)
+    for dr in (1, -1):
+        for c in copies["own", dr]:
+            c.wait_recv()
 
     fill = (zero, one, zero)
 
@@ -132,47 +180,87 @@
         q = row % ROWS
         return from_side[which, kind * 2 + q // 8], from_side[3 + which, kind * 2 + q // 8], 16 * (q % 8)
 
-    def side_tile(kind, j, mains):
+    def side_start(kind, j, mains):
         tile = fill[kind]
+        for g, m in mains.items():
+            own = jnp.where(relx < 64, roll(m, 4), roll(m, -4))
+            tile = jnp.where((band == g) & edge, own, tile)
+        return tile
+
+    def side_tile(kind, j, tile):
         for g in range(3):
             row = FIRST_ROW[g] + j
             if row not in K_ROWS[g] or (kind and not 0 <= j < LENGTH[g]):
                 continue
-            in_core = (row < 0, 0 <= row < ROWS, row >= ROWS)[g]
-            if kind == 2 and not in_core:
+            if kind == 2 and not (row < 0, 0 <= row < ROWS, row >= ROWS)[g]:
                 continue
-            at = g * COLS
             w, e, off = strips(kind, row)
             part = jnp.where(relx < 64, roll(e, 4 + SKEW[g] - off), roll(w, SKEW[g] - 18 - off))
-            if kind == 2:
-                keep = ((code >= at + 4) & (code < at + 18)) | ((code >= at + 110) & (code < at + 124))
-                part = jnp.where(keep, part, 0.0)
-            else:
-                m = mains[g]
-                own = jnp.where(relx < 64, roll(m, 4), roll(m, -4))
-                part = jnp.where((relx < 4) | (relx >= 124), own, part)
             exists = has_n if row < 0 else (has_s if row >= ROWS else None)
             if exists is not None:
                 part = jnp.where(exists, part, fill[kind])
-            tile = jnp.where((band == g) & mine_any, part, tile)
+            tile = jnp.where((band == g) & strip, part, tile)
         if kind != 2:
             tile = jnp.where(relx < 2, roll(tile, -4), jnp.where(relx >= 126, roll(tile, 4), tile))
-            tile = jnp.where(mine_any, tile, fill[kind])
-        return tile
+        return jnp.where(mine_any, tile, fill[kind])
 
     mine_any = mine[0] | mine[1] | mine[2]
+    edge = mine_any & ((relx == 2) | (relx == 3) | (relx == 124) | (relx == 125))
+    strip = mine_any & (((relx >= 4) & (relx < 18)) | ((relx >= 110) & (relx < 124)))
 
     def hidx(g, j):
         return (0, 16, 36)[g] + j + (1 if g == 0 else 0)
 
-    for j in range(-1, 20):
+    def conduct_tiles(j):
         mains = {}
         for g in range(3):
             row = FIRST_ROW[g] + j
             if row in K_ROWS[g]:
                 mains[g] = roll(main_row(0, row), SKEW[g])
                 half[hidx(g, j)] = 0.5 * mains[g]
-        half_side[j + 1] = 0.5 * side_tile(0, j, mains)
+        half_side[j + 1] = side_start(0, j, mains)
+
+    blocks(range(-1, 20), CHUNK[0], conduct_tiles)
+
+    top, bottom = level == NZ - 1, level == 0
+
+    def vertical(h):
+        return h + jnp.where(top, 0.0, vroll(h, -1)), h + jnp.where(bottom, 0.0, vroll(h, 1))
+
+    def main_tiles(j):
+        shifts = {}
+        for g in range(3):
+            if j >= LENGTH[g]:
+                continue
+            row, at = FIRST_ROW[g] + j, BASE[g] + j
+            shifts[g] = s = roll(main_row(1, row), SKEW[g])
+            h = half[hidx(g, j)]
+            vp, vm = vertical(h)
+            rp = h + (half[hidx(g, j + 1)] if row + 1 in K_ROWS[g] else zero)
+            rm = h + (half[hidx(g, j - 1)] if row - 1 in K_ROWS[g] else zero)
+            est[at] = (((s + vp) + vm) + rp) + rm
+            wgt[0, at] = jnp.where(top, 0.0, vp)
+            wgt[1, at] = jnp.where(bottom, 0.0, vm)
+            wgt[2, at] = rp
+            wgt[3, at] = rm
+            if (row < 0, 0 <= row < ROWS, row >= ROWS)[g]:
+                rhs[at] = roll(main_row(2, row), SKEW[g])
+            else:
+                rhs[at] = zero
+        est[SIDE + j] = side_start(1, j, shifts)
+
+    blocks(range(20), CHUNK[1], main_tiles)
+
+    for w in ways:
+        if w[0] != "own":
+            for c in copies[w]:
+                c.wait_recv()
+    copies = [c for w in ways for c in copies[w]]
+
+    def conduct_side_tiles(j):
+        half_side[j + 1] = 0.5 * side_tile(0, j, half_side[j + 1])
+
+    blocks(range(-1, 20), CHUNK[5], conduct_side_tiles)
 
     def around_cols(mains, side):
         sp, sm = roll(side, -1), roll(side, 1)
@@ -185,60 +273,51 @@
         out[3] = (plus, minus)
         return out
 
-    top, bottom = level == NZ - 1, level == 0
     no_plus = (relx == 1) | (relx == 125)
     no_minus = (relx == 2) | (relx == 126)
     live = mine_any & ((relx < 17) | (relx > 110))
 
-    def weights(at, h, s, up, down, plus, minus, side, alive):
-        vp = h + jnp.where(top, 0.0, vroll(h, -1))
-        vm = h + jnp.where(bottom, 0.0, vroll(h, 1))
-        rp = h + down
+    tau0 = TAUS[0]
+
+    def weight_tiles(j):
+        bands = [g for g in range(3) if j < LENGTH[g]]
+        mains = {g: half[hidx(g, j)] for g in bands}
+        h = half_side[j + 1]
+        cols = around_cols(mains, h)
+        for g in bands:
+            at = BASE[g] + j
+            cp, cm = mains[g] + cols[g][0], mains[g] + cols[g][1]
+            inverse = 1.0 / ((est[at] + cp) + cm)
+            for i in range(4):
+                wgt[i, at] = inverse * wgt[i, at]
+            wgt[4, at] = inverse * cp
+            wgt[5, at] = inverse * cm
+            b = inverse * rhs[at]
+            rhs[at] = b
+            est[at] = tau0 * b
+        at = SIDE + j
+        up = half_side[j]
+        if j == 0:
+            up = jnp.where(band == 0, up, 0.0)
+        vp, vm = vertical(h)
+        rp = h + (half_side[j + 2] if j < 19 else zero)
         rm = h + up
-        cp = h + (jnp.where(no_plus, 0.0, plus) if side else plus)
-        cm = h + (jnp.where(no_minus, 0.0, minus) if side else minus)
-        inverse = 1.0 / ((((((s + vp) + vm) + rp) + rm) + cp) + cm)
-        if side:
-            inverse = jnp.where(alive, inverse, 0.0)
+        cp = h + jnp.where(no_plus, 0.0, cols[3][0])
+        cm = h + jnp.where(no_minus, 0.0, cols[3][1])
+        inverse = 1.0 / ((((((side_tile(1, j, est[at]) + vp) + vm) + rp) + rm) + cp) + cm)
+        alive = live if len(bands) == 3 else live & (band == 1)
+        inverse = jnp.where(alive, inverse, 0.0)
         wgt[0, at] = jnp.where(top, 0.0, inverse * vp)
         wgt[1, at] = jnp.where(bottom, 0.0, inverse * vm)
         wgt[2, at] = inverse * rp
         wgt[3, at] = inverse * rm
-        cp, cm = inverse * cp, inverse * cm
-        wgt[4, at] = jnp.where(no_plus, 0.0, cp) if side else cp
-        wgt[5, at] = jnp.where(no_minus, 0.0, cm) if side else cm
-        return inverse
-
-    tau0 = TAUS[0]
-    for j in range(20):
-        bands = [g for g in range(3) if j < LENGTH[g]]
-        mains = {g: half[hidx(g, j)] for g in bands}
-        side = half_side[j + 1]
-        cols = around_cols(mains, side)
-        shifts = {}
-        for g in bands:
-            row = FIRST_ROW[g] + j
-            shifts[g] = roll(main_row(1, row), SKEW[g])
-            up = half[hidx(g, j - 1)] if row - 1 in K_ROWS[g] else zero
-            down = half[hidx(g, j + 1)] if row + 1 in K_ROWS[g] else zero
-            inverse = weights(BASE[g] + j, mains[g], shifts[g], up, down, *cols[g], False, None)
-            if (row < 0, 0 <= row < ROWS, row >= ROWS)[g]:
-                b = inverse * roll(main_row(2, row), SKEW[g])
-            else:
-                b = zero
-            rhs[BASE[g] + j] = b
-            est[BASE[g] + j] = tau0 * b
-        alive = live
-        if len(bands) == 1:
-            alive = live & (band == 1)
-        up = half_side[j]
-        if j == 0:
-            up = jnp.where(band == 0, up, 0.0)
-        down = half_side[j + 2] if j < 19 else zero
-        inverse = weights(SIDE + j, side, side_tile(1, j, shifts), up, down, *cols[3], True, alive)
-        b = inverse * side_tile(2, j, None)
-        rhs[SIDE + j] = b
-        est[SIDE + j] = tau0 * b
+        wgt[4, at] = jnp.where(no_plus, 0.0, inverse * cp)
+        wgt[5, at] = jnp.where(no_minus, 0.0, inverse * cm)
+        b = inverse * side_tile(2, j, zero)
+        rhs[at] = b
+        est[at] = tau0 * b
+
+    blocks(range(20), CHUNK[1], weight_tiles)
 
     def stencil(ref, b, spans, emit):
         def load(g, j):
@@ -311,7 +390,7 @@
     from_plus = (relx == 122) | (relx == 123) | (relx == 0) | (relx == 1)
     from_main_minus = (relx == 2) | (relx == 3)
     from_main_plus = (relx == 124) | (relx == 125)
-    for j in range(20):
+    def first_tiles(j):
         side = gather_rows_side(j)
         s4, s_4 = roll(side, 4), roll(side, -4)
         add = jnp.where(from_minus, s4, jnp.where(from_plus, s_4, 0.0))
@@ -330,6 +409,8 @@
         if exists is not None:
             f = jnp.where((band != 1) | exists, f, 0.0)
         first[SIDE + j] = f
+
+    blocks(range(20), CHUNK[2], first_tiles)
 
     core_lane = ((relx >= 4) & (relx < 17)) | ((relx > 110) & (relx < 124))
 
@@ -360,11 +441,11 @@
         rhs[at] = b
         est[at] = tau0 * b
 
-    stencil(first, rhs, near, emit_rhs)
+    blocks([0], 1, lambda _: stencil(first, rhs, near, emit_rhs))
 
     solve([range(7, 15), range(0, 20), range(0, 8)])
 
-    for j in range(2, 18):
+    def out_rows(j):
         side = est[SIDE + j]
         if j < 4:
             side = side + roll(est[SIDE + j + 11], -SKEW[0])
@@ -373,6 +454,8 @@
         v = first[BASE[1] + j] + gather_rows(1, j)
         v = v + jnp.where(lane < 2, roll(side, 4), jnp.where(lane >= 126, roll(side, -4), 0.0))
         out_ref[pl.ds(j - 2, NZ, stride=ROWS), :] = v
+
+    blocks(range(2, 18), CHUNK[3], out_rows)
 
     for c in copies:
         c.wait_send()
@@ -396,6 +479,7 @@
             pltpu.VMEM((6, TILES, *tile), f32),
             pltpu.VMEM((TILES, *tile), f32), pltpu.VMEM((TILES, *tile), f32), pltpu.VMEM((TILES, *tile), f32),
             pltpu.SemaphoreType.DMA((3,)), pltpu.SemaphoreType.DMA((12,)), pltpu.SemaphoreType.DMA((12,)),
+            pltpu.SemaphoreType.REGULAR((8,)),
         ],
         compiler_params=pltpu.CompilerParams(
             collective_id=0, has_side_effects=True, vmem_limit_bytes=16 * 1024 * 1024),

time: 39.9 us -> 30 us (0.75)
  Pallas kernels: 39.1 us -> 29.2 us
    pallas_call x1, Pallas kernels: 39.1 us -> 29.2 us  [body(): pl.pallas_call(kernel, out_shape=jax.ShapeDtypeStruct(flat, f32), in_spec...]
where the time goes in v2:
time: 30 us; the launch traced here: 29.8 us
  Pallas kernels  29.2 us (97%)
  local copies, waits for them, and re-layouts  0.63 us (2%)
    pallas_call x1, Pallas kernels, body(): pl.pallas_call(kernel, out_shape=jax.ShapeDtypeStruct(flat, f32), in_spec...  29.2 us
    unnamed x1, local copies, waits for them, and re-layouts  0.63 us

profile of v2, /device:TPU:1, one launch (start us, length us, event | category | flops | bytes accessed | tf_op | source)
XLA Modules:
  0.0 29.8 jit_solution(16688083145496918078)
XLA Ops:
  0.0 29.2 %shard_map.37 = f32[128,128]{1,0:T(8,128)S(1)} custom-call(f32[128,128]{1,0:T(8,128)} %bitcast.5, f32[128,128]{1,0:T(8,128)} %bitcast.6, s32[128,128]{1,0:T(8,128)} %bitcast.7), custom_call_target="tpu_custom_call" | custom-call | tf_op jit(solution)/shard_map/pallas_call | solution.py:468
  29.2 0.6 %copy.5 = f32[8,16,128]{2,1,0:T(8,128)} copy(f32[8,16,128]{2,1,0:T(8,128)S(1)} %bitcast.4) | data formatting | bytes 131072

commit v3 on v2

--- a/solution.py
+++ b/solution.py
@@ -98,8 +98,8 @@
     level = lax.broadcasted_iota(jnp.int32, (NZ, COLS), 0)
     rel = [lax.rem(lane + (COLS - s), COLS) for s in SKEW]
     mine = [(q < 18) | (q >= 110) for q in rel]
-    relx = jnp.where(mine[0], rel[0], jnp.where(mine[2], rel[2], rel[1]))
-    band = jnp.where(mine[0], 0, jnp.where(mine[2], 2, 1))
+    band = jnp.where(mine[0], 0, jnp.where(mine[2], 2, jnp.where(mine[1], 1, 3)))
+    relx = jnp.where(mine[0], rel[0], jnp.where(mine[2], rel[2], jnp.where(mine[1], rel[1], 64)))
     code = band * COLS + relx
     zero = jnp.zeros((NZ, COLS), jnp.float32)
     one = jnp.ones((NZ, COLS), jnp.float32)
@@ -112,11 +112,11 @@
             return 0.05 + 20.0 * own_solid[rows, :].astype(jnp.float32)
         return own_src[rows, :]
 
-    for c in loads:
-        c.wait()
     slot = lax.div(lane, 16)
     def pack(i):
         kind, half_of = divmod(i, 2)
+        if half_of == 0:
+            loads[kind].wait()
         west, east = zero, zero
         for s in range(8):
             v = own_row(kind, half_of * 8 + s)
@@ -175,38 +175,38 @@
             v = ns_src[w, rows, :]
         return jnp.where(exists, v, fill[kind])
 
-    def strips(kind, row):
-        which = 0 if row < 0 else (1 if row < ROWS else 2)
-        q = row % ROWS
-        return from_side[which, kind * 2 + q // 8], from_side[3 + which, kind * 2 + q // 8], 16 * (q % 8)
-
     def side_start(kind, j, mains):
         tile = fill[kind]
         for g, m in mains.items():
             own = jnp.where(relx < 64, roll(m, 4), roll(m, -4))
-            tile = jnp.where((band == g) & edge, own, tile)
+            tile = jnp.where(edge == g, own, tile)
         return tile
 
-    def side_tile(kind, j, tile):
+    def strips(side, kind, j, tile):
         for g in range(3):
             row = FIRST_ROW[g] + j
             if row not in K_ROWS[g] or (kind and not 0 <= j < LENGTH[g]):
                 continue
             if kind == 2 and not (row < 0, 0 <= row < ROWS, row >= ROWS)[g]:
                 continue
-            w, e, off = strips(kind, row)
-            part = jnp.where(relx < 64, roll(e, 4 + SKEW[g] - off), roll(w, SKEW[g] - 18 - off))
-            exists = has_n if row < 0 else (has_s if row >= ROWS else None)
-            if exists is not None:
-                part = jnp.where(exists, part, fill[kind])
-            tile = jnp.where((band == g) & strip, part, tile)
-        if kind != 2:
-            tile = jnp.where(relx < 2, roll(tile, -4), jnp.where(relx >= 126, roll(tile, 4), tile))
-        return jnp.where(mine_any, tile, fill[kind])
-
-    mine_any = mine[0] | mine[1] | mine[2]
-    edge = mine_any & ((relx == 2) | (relx == 3) | (relx == 124) | (relx == 125))
-    strip = mine_any & (((relx >= 4) & (relx < 18)) | ((relx >= 110) & (relx < 124)))
+            which, q = (0 if row < 0 else (1 if row < ROWS else 2)), row % ROWS
+            v = from_side[first_of[side] + which, kind * 2 + q // 8]
+            by = lax.rem(shift_of[side] + (SKEW[g] - 16 * (q % 8) + COLS), COLS)
+            at = g if which == 1 else jnp.where((has_n, None, has_s)[which], g, 8)
+            tile = jnp.where(strip_of[side] == at, pltpu.roll(v, by, 1), tile)
+        return tile
+
+    def finish(tile):
+        return jnp.where(relx < 2, roll(tile, -4), jnp.where(relx >= 126, roll(tile, 4), tile))
+
+    edge = jnp.where((relx == 2) | (relx == 3) | (relx == 124) | (relx == 125), band, 9)
+    east_strip = (relx >= 4) & (relx < 18)
+    west_strip = (relx >= 110) & (relx < 124)
+    east_near = lax.div(near_side + 1, 2)
+    east_of = {"near": east_near, "far": 1 - east_near}
+    first_of = {k: 3 * e for k, e in east_of.items()}
+    shift_of = {k: jnp.where(e == 1, 4, COLS - 18) for k, e in east_of.items()}
+    strip_of = {k: jnp.where((east_strip & (e == 1)) | (west_strip & (e == 0)), band, 9) for k, e in east_of.items()}
 
     def hidx(g, j):
         return (0, 16, 36)[g] + j + (1 if g == 0 else 0)
@@ -221,6 +221,7 @@
         half_side[j + 1] = side_start(0, j, mains)
 
     blocks(range(-1, 20), CHUNK[0], conduct_tiles)
+
 
     top, bottom = level == NZ - 1, level == 0
 
@@ -248,19 +249,38 @@
             else:
                 rhs[at] = zero
         est[SIDE + j] = side_start(1, j, shifts)
+        rhs[SIDE + j] = zero
 
     blocks(range(20), CHUNK[1], main_tiles)
 
-    for w in ways:
-        if w[0] != "own":
-            for c in copies[w]:
+
+    def side_strips(side):
+        def do(j):
+            half_side[j + 1] = strips(side, 0, j, half_side[j + 1])
+            if j >= 0:
+                est[SIDE + j] = strips(side, 1, j, est[SIDE + j])
+                rhs[SIDE + j] = strips(side, 2, j, rhs[SIDE + j])
+        return do
+
+    for side, dr in ways:
+        if side == "near":
+            for c in copies[side, dr]:
+                c.wait_recv()
+    blocks(range(-1, 20), CHUNK[5], side_strips("near"))
+    for side, dr in ways:
+        if side == "far":
+            for c in copies[side, dr]:
                 c.wait_recv()
     copies = [c for w in ways for c in copies[w]]
 
-    def conduct_side_tiles(j):
-        half_side[j + 1] = 0.5 * side_tile(0, j, half_side[j + 1])
-
-    blocks(range(-1, 20), CHUNK[5], conduct_side_tiles)
+    blocks(range(-1, 20), CHUNK[5], side_strips("far"))
+
+    def finish_tiles(j):
+        half_side[j + 1] = 0.5 * finish(half_side[j + 1])
+        if j >= 0:
+            est[SIDE + j] = finish(est[SIDE + j])
+
+    blocks(range(-1, 20), CHUNK[5], finish_tiles)
 
     def around_cols(mains, side):
         sp, sm = roll(side, -1), roll(side, 1)
@@ -275,7 +295,7 @@
 
     no_plus = (relx == 1) | (relx == 125)
     no_minus = (relx == 2) | (relx == 126)
-    live = mine_any & ((relx < 17) | (relx > 110))
+    live = (band < 3) & ((relx < 17) | (relx > 110))
 
     tau0 = TAUS[0]
 
@@ -304,16 +324,15 @@
         rm = h + up
         cp = h + jnp.where(no_plus, 0.0, cols[3][0])
         cm = h + jnp.where(no_minus, 0.0, cols[3][1])
-        inverse = 1.0 / ((((((side_tile(1, j, est[at]) + vp) + vm) + rp) + rm) + cp) + cm)
-        alive = live if len(bands) == 3 else live & (band == 1)
-        inverse = jnp.where(alive, inverse, 0.0)
+        inverse = 1.0 / ((((((est[at] + vp) + vm) + rp) + rm) + cp) + cm)
+        inverse = jnp.where(live if len(bands) == 3 else live & (band == 1), inverse, 0.0)
         wgt[0, at] = jnp.where(top, 0.0, inverse * vp)
         wgt[1, at] = jnp.where(bottom, 0.0, inverse * vm)
         wgt[2, at] = inverse * rp
         wgt[3, at] = inverse * rm
         wgt[4, at] = jnp.where(no_plus, 0.0, inverse * cp)
         wgt[5, at] = jnp.where(no_minus, 0.0, inverse * cm)
-        b = inverse * side_tile(2, j, zero)
+        b = inverse * rhs[at]
         rhs[at] = b
         est[at] = tau0 * b
 
@@ -383,25 +402,26 @@
             v = v + jnp.where(band == 1, roll(est[SIDE + j - 16], -SKEW[2]), 0.0)
         if 11 <= j < 15:
             v = v + jnp.where(band == 0, roll(est[SIDE + j - 11], SKEW[0]), 0.0)
-        return jnp.where(mine_any, v, 0.0)
+        return v
 
     near = [range(6, 15), range(0, 20), range(0, 9)]
-    from_minus = (relx == 126) | (relx == 127) | (relx == 4) | (relx == 5)
-    from_plus = (relx == 122) | (relx == 123) | (relx == 0) | (relx == 1)
-    from_main_minus = (relx == 2) | (relx == 3)
-    from_main_plus = (relx == 124) | (relx == 125)
+    def among(*values):
+        return functools.reduce(jnp.logical_or, [relx == v for v in values])
+
+    origin = jnp.where(among(126, 127, 4, 5), 1, jnp.where(among(122, 123, 0, 1), 2, jnp.where(among(2, 3), 3, jnp.where(among(124, 125), 4, 0))))
+    crossing = jnp.where(origin >= 3, band, 9)
+
     def first_tiles(j):
         side = gather_rows_side(j)
         s4, s_4 = roll(side, 4), roll(side, -4)
-        add = jnp.where(from_minus, s4, jnp.where(from_plus, s_4, 0.0))
+        add = jnp.where(origin == 1, s4, jnp.where(origin == 2, s_4, 0.0))
         exists = has_n if j < 2 else (has_s if j >= 18 else None)
         for g in range(3):
             if j not in near[g]:
                 continue
             m = gather_rows(g, j)
             f = m + jnp.where(rel[g] < 2, s4, jnp.where(rel[g] >= 126, s_4, 0.0))
-            cross = jnp.where(from_main_minus, roll(m, 4), jnp.where(from_main_plus, roll(m, -4), add))
-            add = jnp.where(band == g, cross, add)
+            add = jnp.where(crossing == g, jnp.where(origin == 3, roll(m, 4), roll(m, -4)), add)
             if g == 1 and exists is not None:
                 f = jnp.where(exists, f, 0.0)
             first[BASE[g] + j] = f
@@ -412,26 +432,20 @@
 
     blocks(range(20), CHUNK[2], first_tiles)
 
-    core_lane = ((relx >= 4) & (relx < 17)) | ((relx > 110) & (relx < 124))
+    core = jnp.where(((relx >= 4) & (relx < 17)) | ((relx > 110) & (relx < 124)), band, 9)
+    to_north, to_south = jnp.where(has_n, 0, 8), jnp.where(has_s, 2, 8)
 
     def emit_rhs(at, g, j, total, x):
         b = total - x
         if g == 3:
-            keep = core_lane & mine_any
             use = []
             if 7 <= j <= 12:
-                use.append((band == 0) & has_n)
+                use.append(core == to_north)
             if 2 <= j <= 17:
-                use.append(band == 1)
+                use.append(core == 1)
             if 2 <= j <= 7:
-                use.append((band == 2) & has_s)
-            if not use:
-                b = zero
-            else:
-                any_use = use[0]
-                for u in use[1:]:
-                    any_use = any_use | u
-                b = jnp.where(keep & any_use, b, 0.0)
+                use.append(core == to_south)
+            b = jnp.where(functools.reduce(jnp.logical_or, use), b, 0.0) if use else zero
         elif g == 0:
             b = jnp.where(has_n, b, 0.0) if 7 <= j <= 12 else zero
         elif g == 2:

time: 30 us -> 29 us (0.967)
  Pallas kernels: 29.2 us -> 28.2 us
    pallas_call x1, Pallas kernels: 29.2 us -> 28.2 us  [body(): pl.pallas_call(kernel, out_shape=jax.ShapeDtypeStruct(flat, f32), in_spec...]
where the time goes in v3:
time: 29 us; the launch traced here: 28.9 us
  Pallas kernels  28.2 us (97%)
  local copies, waits for them, and re-layouts  0.63 us (2%)
    pallas_call x1, Pallas kernels, body(): pl.pallas_call(kernel, out_shape=jax.ShapeDtypeStruct(flat, f32), in_spec...  28.2 us
    unnamed x1, local copies, waits for them, and re-layouts  0.63 us

profile of v3, /device:TPU:1, one launch (start us, length us, event | category | flops | bytes accessed | tf_op | source)
XLA Modules:
  0.0 28.9 jit_solution(2799247774113152480)
XLA Ops:
  0.0 28.2 %shard_map.37 = f32[128,128]{1,0:T(8,128)S(1)} custom-call(f32[128,128]{1,0:T(8,128)} %bitcast.5, f32[128,128]{1,0:T(8,128)} %bitcast.6, s32[128,128]{1,0:T(8,128)} %bitcast.7), custom_call_target="tpu_custom_call" | custom-call | tf_op jit(solution)/shard_map/pallas_call | solution.py:482
  28.2 0.6 %copy.5 = f32[8,16,128]{2,1,0:T(8,128)} copy(f32[8,16,128]{2,1,0:T(8,128)S(1)} %bitcast.4) | data formatting | bytes 131072

commit v4 on v3

--- a/solution.py
+++ b/solution.py
@@ -364,7 +364,7 @@
                 other = other + wgt[5, at] * minus
                 emit(at, g, j, total + other, x)
 
-    def solve(spans):
+    def solve(spans, begin, end):
         def sweep(t, carry):
             tau = jnp.float32(TAUS[STEPS - 1])
             for i in range(STEPS - 2, 0, -1):
@@ -376,10 +376,11 @@
             stencil(est, rhs, spans, emit)
             return carry
 
-        lax.fori_loop(1, STEPS, sweep, 0)
+        lax.fori_loop(begin, end, sweep, 0)
 
     full = [range(n) for n in LENGTH]
-    solve(full)
+    solve(full, 1, 4)
+    solve([range(3, 15), range(0, 20), range(0, 12)], 4, STEPS)
 
     def gather_rows(g, j):
         v = est[BASE[g] + j]
@@ -457,7 +458,8 @@
 
     blocks([0], 1, lambda _: stencil(first, rhs, near, emit_rhs))
 
-    solve([range(7, 15), range(0, 20), range(0, 8)])
+    solve([range(7, 15), range(0, 20), range(0, 8)], 1, 4)
+    solve([range(10, 15), range(0, 20), range(0, 5)], 4, STEPS)
 
     def out_rows(j):
         side = est[SIDE + j]

time: 29 us -> 29 us (level)
  no operation moved by 1% of the time
where the time goes in v4:
time: 29 us; the launch traced here: 28.8 us
  Pallas kernels  28.1 us (97%)
  local copies, waits for them, and re-layouts  0.63 us (2%)
    pallas_call x1, Pallas kernels, body(): pl.pallas_call(kernel, out_shape=jax.ShapeDtypeStruct(flat, f32), in_spec...  28.1 us
    unnamed x1, local copies, waits for them, and re-layouts  0.63 us

profile of v4, /device:TPU:1, one launch (start us, length us, event | category | flops | bytes accessed | tf_op | source)
XLA Modules:
  0.0 28.8 jit_solution(13167676566625420088)
XLA Ops:
  0.0 28.1 %shard_map.37 = f32[128,128]{1,0:T(8,128)S(1)} custom-call(f32[128,128]{1,0:T(8,128)} %bitcast.5, f32[128,128]{1,0:T(8,128)} %bitcast.6, s32[128,128]{1,0:T(8,128)} %bitcast.7), custom_call_target="tpu_custom_call" | custom-call | tf_op jit(solution)/shard_map/pallas_call | solution.py:484
  28.1 0.6 %copy.5 = f32[8,16,128]{2,1,0:T(8,128)} copy(f32[8,16,128]{2,1,0:T(8,128)S(1)} %bitcast.4) | data formatting | bytes 131072
